TPU v7x, 32 devices: a whole 2x2x4 slice. The times are simulated.
32 devices in a mesh: dp: 8 (over z, y), mp: 4 (over x, core).
Axes of the slice: x: 2, y: 2, z: 4, core: 2. Of those that a mesh axis runs over, the one named last changes fastest.
Arguments:
- tokens: bfloat16 [4096, 2048], P('dp'), may hold values from -6 to 6
- text: bfloat16 [2048, 4096], P('dp', 'mp'), may hold values from -6 to 6
- image_seg: int32 [8, 512], P('dp'), may hold values from 0 to 1, never falling along the last dimension, each value on 1 to 320 neighbouring positions
- text_seg: int32 [8, 256], P('dp'), may hold values from 0 to 1, never falling along the last dimension, each value on 1 to 160 neighbouring positions
- w_qkv: bfloat16 [3, 2048, 2048], P(None, 'dp', 'mp'), may hold values from -0.125 to 0.125
- w_out: bfloat16 [2048, 2048], P('mp', 'dp'), may hold values from -1 to 1
- c_q: bfloat16 [2048, 2048], P('dp', 'mp'), may hold values from -0.125 to 0.125
- c_kv: bfloat16 [2, 4096, 2048], P(None, 'dp', 'mp'), may hold values from -0.09375 to 0.09375
- c_out: bfloat16 [2048, 2048], P('mp', 'dp'), may hold values from -1 to 1
- w_up: bfloat16 [2048, 8192], P('dp', 'mp'), may hold values from -0.125 to 0.125
- w_down: bfloat16 [8192, 2048], P('mp', 'dp'), may hold values from -0.0625 to 0.0625
- norm_gain: float32 [4, 2048], replicated, may hold values from 0.25 to 1.75
- norm_bias: float32 [4, 2048], replicated, may hold values from -4 to 4
- out_bias: float32 [3, 2048], replicated, may hold values from -4 to 4
- up_bias: float32 [8192], P('mp'), may hold values from -4 to 4
- cotangent: bfloat16 [4096, 2048], P('dp'), may hold values from -6 to 6
Outputs:
- output: bfloat16 [4096, 2048], P('dp')
- grad_tokens: float32 [4096, 2048], P('dp')
- grad_text: float32 [2048, 4096], P('dp', 'mp')
- grad_w_qkv: float32 [3, 2048, 2048], P(None, 'dp', 'mp')
- grad_w_out: float32 [2048, 2048], P('mp', 'dp')
- grad_c_q: float32 [2048, 2048], P('dp', 'mp')
- grad_c_kv: float32 [2, 4096, 2048], P(None, 'dp', 'mp')
- grad_c_out: float32 [2048, 2048], P('mp', 'dp')
- grad_w_up: float32 [2048, 8192], P('dp', 'mp')
- grad_w_down: float32 [8192, 2048], P('mp', 'dp')
- grad_norm_gain: float32 [4, 2048], replicated
- grad_norm_bias: float32 [4, 2048], replicated
- grad_out_bias: float32 [3, 2048], replicated
- grad_up_bias: float32 [8192], P('mp')
Inputs may be any that keep to these rules, and one draw needn't show every extreme that they name: In each row image_seg is 0 on the first image and 1 on the second; both images are present, and none has more than 320 tokens. In each row text_seg is 0 on the first caption and 1 on the second; both captions are present, and none has more than 160 tokens.
All inputs are finite; a program needn't handle non-finite values.
Results may differ from a plain program's by a relative error of at most 0.02.
Values may be sent and summed in bfloat16 or wider, within the bound.
No kernel may reach another device: no remote copies, remote signals or barrier semaphores. Data moves between devices by JAX's collectives and lax.ppermute only.
A program may use at most 256 MiB of HBM per device.

v0:
```python
import jax
import jax.numpy as jnp
from jax import lax
from jax.sharding import PartitionSpec as P

HD = 128
eps = 1e-05
masked = -1e30


def normalize(values, gain, shift):
    center = values - jnp.mean(values, axis=-1, keepdims=True)
    spread = jnp.mean(center * center, axis=-1, keepdims=True)
    return center * lax.rsqrt(spread + eps) * gain + shift


def gelu_tanh(values):
    return (
        0.5
        * values
        * (1.0 + jnp.tanh(0.7978845608028654 * (values + 0.044715 * values * values * values)))
    )


def heads_sum(partial_value):
    return lax.psum(partial_value, "mp")


def input_sum(partial_value):
    return lax.psum(partial_value, "mp")


def split_heads(values):
    return values.reshape(values.shape[0], values.shape[1] // HD, HD)


def scores_of(queries, key_rows, allowed):
    raw = jnp.einsum(
        "qhd,khd->hqk",
        split_heads(queries),
        split_heads(key_rows),
        preferred_element_type=jnp.float32,
    ) * HD ** (-0.5)
    return jnp.where(allowed[None], raw, masked)


def attend_forward(queries, key_rows, value_rows, allowed):
    scores = scores_of(queries, key_rows, allowed)
    top = jnp.max(scores, axis=-1, keepdims=True)
    expo = jnp.exp(scores - top)
    total = jnp.sum(expo, axis=-1, keepdims=True)
    probs = (expo / total).astype(jnp.bfloat16)
    mixed = jnp.einsum(
        "hqk,khd->qhd", probs, split_heads(value_rows), preferred_element_type=jnp.float32
    )
    return (
        mixed.reshape(queries.shape[0], queries.shape[1]).astype(jnp.bfloat16),
        top + jnp.log(total),
    )


def attend_backward(queries, key_rows, value_rows, grad_mixed, logsum, allowed):
    scores = scores_of(queries, key_rows, allowed)
    probs = jnp.exp(scores - logsum)
    grad_heads = split_heads(grad_mixed)
    grad_values = jnp.einsum(
        "hqk,qhd->khd", probs.astype(jnp.bfloat16), grad_heads, preferred_element_type=jnp.float32
    )
    grad_probs = jnp.einsum(
        "qhd,khd->hqk", grad_heads, split_heads(value_rows), preferred_element_type=jnp.float32
    )
    grad_scores = (
        probs * (grad_probs - jnp.sum(probs * grad_probs, axis=-1, keepdims=True))
    ).astype(jnp.bfloat16)
    grad_queries = jnp.einsum(
        "hqk,khd->qhd", grad_scores, split_heads(key_rows), preferred_element_type=jnp.float32
    ) * HD ** (-0.5)
    grad_keys = jnp.einsum(
        "hqk,qhd->khd", grad_scores, split_heads(queries), preferred_element_type=jnp.float32
    ) * HD ** (-0.5)
    return (
        grad_queries.reshape(queries.shape),
        grad_keys.reshape(key_rows.shape),
        grad_values.reshape(value_rows.shape),
    )


def on_device(
    tokens,
    text,
    image_seg,
    text_seg,
    w_qkv,
    w_out,
    c_q,
    c_kv,
    c_out,
    w_up,
    w_down,
    norm_gain,
    norm_bias,
    out_bias,
    up_bias,
    cotangent,
):
    row_count = image_seg.shape[0]
    length = image_seg.shape[1]
    text_len = text_seg.shape[1]
    gathered = (
        lax.all_gather(w_qkv, "dp", axis=1, tiled=True),
        lax.all_gather(w_out, "dp", axis=1, tiled=True),
        lax.all_gather(c_q, "dp", axis=0, tiled=True),
        lax.all_gather(c_kv, "dp", axis=1, tiled=True),
        lax.all_gather(c_out, "dp", axis=1, tiled=True),
        lax.all_gather(w_up, "dp", axis=0, tiled=True),
        lax.all_gather(w_down, "dp", axis=1, tiled=True),
    )
    full_qkv, full_out, full_cq, full_ckv, full_cout, full_up, full_down = gathered
    words = lax.all_gather(text, "mp", axis=1, tiled=True)
    same_image = image_seg[:, :, None] == image_seg[:, None, :]
    caption = image_seg[:, :, None] == text_seg[:, None, :]
    residual = tokens.astype(jnp.float32)
    width = full_qkv.shape[2]
    normed_one, pull_one = jax.vjp(normalize, residual, norm_gain[0], norm_bias[0])
    hidden_one = normed_one.astype(jnp.bfloat16)
    projected = jnp.einsum(
        "td,cde->cte", hidden_one, full_qkv, preferred_element_type=jnp.float32
    ).astype(jnp.bfloat16)
    self_inputs = (
        projected[0].reshape(row_count, length, width),
        projected[1].reshape(row_count, length, width),
        projected[2].reshape(row_count, length, width),
    )
    self_mixed, self_logsum = lax.map(
        lambda pieces: attend_forward(*pieces), self_inputs + (same_image,)
    )
    self_flat = self_mixed.reshape(row_count * length, width)
    after_self = (
        residual
        + heads_sum(jnp.dot(self_flat, full_out, preferred_element_type=jnp.float32))
        + out_bias[0]
    )
    normed_two, pull_two = jax.vjp(normalize, after_self, norm_gain[1], norm_bias[1])
    hidden_two = normed_two.astype(jnp.bfloat16)
    cross_query = jnp.dot(hidden_two, full_cq, preferred_element_type=jnp.float32).astype(
        jnp.bfloat16
    )
    text_kv = jnp.einsum("td,cde->cte", words, full_ckv, preferred_element_type=jnp.float32).astype(
        jnp.bfloat16
    )
    cross_inputs = (
        cross_query.reshape(row_count, length, width),
        text_kv[0].reshape(row_count, text_len, width),
        text_kv[1].reshape(row_count, text_len, width),
    )
    cross_mixed, cross_logsum = lax.map(
        lambda pieces: attend_forward(*pieces), cross_inputs + (caption,)
    )
    cross_flat = cross_mixed.reshape(row_count * length, width)
    after_cross = (
        after_self
        + heads_sum(jnp.dot(cross_flat, full_cout, preferred_element_type=jnp.float32))
        + out_bias[1]
    )
    normed_three, pull_three = jax.vjp(normalize, after_cross, norm_gain[2], norm_bias[2])
    hidden_three = normed_three.astype(jnp.bfloat16)
    pre_act = jnp.dot(hidden_three, full_up, preferred_element_type=jnp.float32) + up_bias
    activated, pull_gelu = jax.vjp(gelu_tanh, pre_act)
    act_low = activated.astype(jnp.bfloat16)
    after_mlp = (
        after_cross
        + heads_sum(jnp.dot(act_low, full_down, preferred_element_type=jnp.float32))
        + out_bias[2]
    )
    final, pull_four = jax.vjp(normalize, after_mlp, norm_gain[3], norm_bias[3])
    output = final.astype(jnp.bfloat16)
    grad_mlp, gain_four, shift_four = pull_four(cotangent.astype(jnp.float32))
    grad_mlp_low = grad_mlp.astype(jnp.bfloat16)
    grad_down = jnp.einsum("tf,td->fd", act_low, grad_mlp_low, preferred_element_type=jnp.float32)
    grad_act = jnp.einsum("td,fd->tf", grad_mlp_low, full_down, preferred_element_type=jnp.float32)
    grad_pre = pull_gelu(grad_act)[0].astype(jnp.bfloat16)
    up_bias_grad = jnp.sum(grad_pre.astype(jnp.float32), axis=0)
    grad_up = jnp.einsum("td,tf->df", hidden_three, grad_pre, preferred_element_type=jnp.float32)
    grad_hidden_three = input_sum(
        jnp.einsum("tf,df->td", grad_pre, full_up, preferred_element_type=jnp.float32)
    )
    grad_cross_in, gain_three, shift_three = pull_three(grad_hidden_three)
    grad_after_cross = grad_mlp + grad_cross_in
    grad_cross_low = grad_after_cross.astype(jnp.bfloat16)
    grad_cout = jnp.einsum(
        "te,td->ed", cross_flat, grad_cross_low, preferred_element_type=jnp.float32
    )
    grad_cmix = jnp.einsum(
        "td,ed->te", grad_cross_low, full_cout, preferred_element_type=jnp.float32
    ).astype(jnp.bfloat16)
    cq_grad, ck_grad, cv_grad = lax.map(
        lambda pieces: attend_backward(*pieces),
        cross_inputs + (grad_cmix.reshape(row_count, length, width), cross_logsum, caption),
    )
    cq_low = cq_grad.reshape(row_count * length, width).astype(jnp.bfloat16)
    ckv_low = jnp.stack(
        [ck_grad.reshape(row_count * text_len, width), cv_grad.reshape(row_count * text_len, width)]
    ).astype(jnp.bfloat16)
    grad_cq = jnp.einsum("td,te->de", hidden_two, cq_low, preferred_element_type=jnp.float32)
    grad_ckv = jnp.einsum("td,cte->cde", words, ckv_low, preferred_element_type=jnp.float32)
    text_term = jnp.einsum("cte,cde->td", ckv_low, full_ckv, preferred_element_type=jnp.float32)
    grad_text = lax.psum_scatter(
        text_term.astype(jnp.bfloat16), "mp", scatter_dimension=1, tiled=True
    ).astype(jnp.float32)
    grad_hidden_two = input_sum(
        jnp.einsum("te,de->td", cq_low, full_cq, preferred_element_type=jnp.float32)
    )
    grad_self_in, gain_two, shift_two = pull_two(grad_hidden_two)
    grad_after_self = grad_after_cross + grad_self_in
    grad_self_low = grad_after_self.astype(jnp.bfloat16)
    grad_wout = jnp.einsum(
        "te,td->ed", self_flat, grad_self_low, preferred_element_type=jnp.float32
    )
    grad_smix = jnp.einsum(
        "td,ed->te", grad_self_low, full_out, preferred_element_type=jnp.float32
    ).astype(jnp.bfloat16)
    sq_grad, sk_grad, sv_grad = lax.map(
        lambda pieces: attend_backward(*pieces),
        self_inputs + (grad_smix.reshape(row_count, length, width), self_logsum, same_image),
    )
    qkv_low = jnp.stack(
        [
            sq_grad.reshape(row_count * length, width),
            sk_grad.reshape(row_count * length, width),
            sv_grad.reshape(row_count * length, width),
        ]
    ).astype(jnp.bfloat16)
    grad_qkv = jnp.einsum("td,cte->cde", hidden_one, qkv_low, preferred_element_type=jnp.float32)
    grad_hidden_one = input_sum(
        jnp.einsum("cte,cde->td", qkv_low, full_qkv, preferred_element_type=jnp.float32)
    )
    grad_in_one, gain_one, shift_one = pull_one(grad_hidden_one)
    grad_tokens = grad_after_self + grad_in_one
    gain_terms = jnp.stack([gain_one, gain_two, gain_three, gain_four])
    shift_terms = jnp.stack([shift_one, shift_two, shift_three, shift_four])
    bias_terms = jnp.stack(
        [
            jnp.sum(grad_after_self, axis=0),
            jnp.sum(grad_after_cross, axis=0),
            jnp.sum(grad_mlp, axis=0),
        ]
    )
    gain_total, shift_total, bias_total, up_total = (
        lax.psum(gain_terms.astype(jnp.bfloat16), "dp").astype(jnp.float32),
        lax.psum(shift_terms.astype(jnp.bfloat16), "dp").astype(jnp.float32),
        lax.psum(bias_terms.astype(jnp.bfloat16), "dp").astype(jnp.float32),
        lax.psum(up_bias_grad.astype(jnp.bfloat16), "dp").astype(jnp.float32),
    )
    sum_qkv, sum_wout, sum_cq, sum_ckv, sum_cout, sum_up, sum_down = (
        lax.psum_scatter(
            grad_qkv.astype(jnp.bfloat16), "dp", scatter_dimension=1, tiled=True
        ).astype(jnp.float32),
        lax.psum_scatter(
            grad_wout.astype(jnp.bfloat16), "dp", scatter_dimension=1, tiled=True
        ).astype(jnp.float32),
        lax.psum_scatter(
            grad_cq.astype(jnp.bfloat16), "dp", scatter_dimension=0, tiled=True
        ).astype(jnp.float32),
        lax.psum_scatter(
            grad_ckv.astype(jnp.bfloat16), "dp", scatter_dimension=1, tiled=True
        ).astype(jnp.float32),
        lax.psum_scatter(
            grad_cout.astype(jnp.bfloat16), "dp", scatter_dimension=1, tiled=True
        ).astype(jnp.float32),
        lax.psum_scatter(
            grad_up.astype(jnp.bfloat16), "dp", scatter_dimension=0, tiled=True
        ).astype(jnp.float32),
        lax.psum_scatter(
            grad_down.astype(jnp.bfloat16), "dp", scatter_dimension=1, tiled=True
        ).astype(jnp.float32),
    )
    return (
        output,
        grad_tokens,
        grad_text,
        sum_qkv,
        sum_wout,
        sum_cq,
        sum_ckv,
        sum_cout,
        sum_up,
        sum_down,
        gain_total,
        shift_total,
        bias_total,
        up_total,
    )


def solution(mesh):
    in_specs = (
        P("dp", None),
        P("dp", "mp"),
        P("dp", None),
        P("dp", None),
        P(None, "dp", "mp"),
        P("mp", "dp"),
        P("dp", "mp"),
        P(None, "dp", "mp"),
        P("mp", "dp"),
        P("dp", "mp"),
        P("mp", "dp"),
        P(),
        P(),
        P(),
        P("mp"),
        P("dp", None),
    )
    out_specs = (
        P("dp", None),
        P("dp", None),
        P("dp", "mp"),
        P(None, "dp", "mp"),
        P("mp", "dp"),
        P("dp", "mp"),
        P(None, "dp", "mp"),
        P("mp", "dp"),
        P("dp", "mp"),
        P("mp", "dp"),
        P(),
        P(),
        P(),
        P("mp"),
    )
    return jax.shard_map(
        on_device, mesh=mesh, in_specs=in_specs, out_specs=out_specs, check_vma=False
    )
```

profile of v0, /device:TPU:0, one launch (start us, length us, event | category | flops | bytes accessed | tf_op | source)
XLA Modules:
  0.0 2109.8 jit_solution(6485817762568258638)
XLA Ops:
  13.9 99.0 %all-gather.9.cloned.1.call-done = bf16[3,2048,512]{1,2,0:T(8,128)(2,1)} async-done(((bf16[3,256,512]{1,2,0:T(8,128)(2,1)}), bf16[3,2048,512]{1,2,0:T(8,128)(2,1)}) %all-gather.9.cloned.1.call-update) | async-done | bytes 6291472 | tf_op jit(solution)/shard_map/all_gather | solution.py:110
  124.3 39.2 %all-gather.11.cloned.1.call-done = bf16[512,2048]{1,0:T(8,128)(2,1)} async-done(((bf16[512,256]{1,0:T(8,128)(2,1)}), bf16[512,2048]{1,0:T(8,128)(2,1)}) %all-gather.11.cloned.1.call-update) | async-done | bytes 2097168 | tf_op jit(solution)/shard_map/all_gather | solution.py:111
  172.5 79.7 %all-reduce.8.cloned.1.call-done = f32[512,2048]{1,0:T(8,128)} async-done(((f32[512,2048]{1,0:T(8,128)}), f32[512,2048]{1,0:T(8,128)}) %all-reduce.8.cloned.1.call-update) | async-done | bytes 4194320 | tf_op jit(solution)/shard_map/psum | solution.py:26
  257.8 45.6 %all-gather.17.cloned.1.call-done = bf16[2048,512]{1,0:T(8,128)(2,1)} async-done(((bf16[256,512]{1,0:T(8,128)(2,1)}), bf16[2048,512]{1,0:T(8,128)(2,1)}) %all-gather.17.cloned.1.call-update) | async-done | bytes 2097168 | tf_op jit(solution)/shard_map/all_gather | solution.py:112
  306.4 19.6 all-gather.15.cloned.1.call-done
  326.0 127.4 %all-gather.13.cloned.1.call-done = bf16[2,4096,512]{1,2,0:T(8,128)(2,1)} async-done(((bf16[2,512,512]{1,2,0:T(8,128)(2,1)}), bf16[2,4096,512]{1,2,0:T(8,128)(2,1)}) %all-gather.13.cloned.1.call-update) | async-done | bytes 8388624 | tf_op jit(solution)/shard_map/all_gather | solution.py:113
  461.3 42.8 %all-gather.19.cloned.1.call-done = bf16[512,2048]{1,0:T(8,128)(2,1)} async-done(((bf16[512,256]{1,0:T(8,128)(2,1)}), bf16[512,2048]{1,0:T(8,128)(2,1)}) %all-gather.19.cloned.1.call-update) | async-done | bytes 2097168 | tf_op jit(solution)/shard_map/all_gather | solution.py:114
  510.5 82.3 %all-reduce.10.cloned.1.call-done = f32[512,2048]{1,0:T(8,128)} async-done(((f32[512,2048]{1,0:T(8,128)}), f32[512,2048]{1,0:T(8,128)}) %all-reduce.10.cloned.1.call-update) | async-done | bytes 4194320 | tf_op jit(solution)/shard_map/psum | solution.py:26
  599.3 120.2 %all-gather.21.cloned.1.call-done = bf16[2048,2048]{1,0:T(8,128)(2,1)} async-done(((bf16[256,2048]{1,0:T(8,128)(2,1)}), bf16[2048,2048]{1,0:T(8,128)(2,1)}) %all-gather.21.cloned.1.call-update) | async-done | bytes 8388624 | tf_op jit(solution)/shard_map/all_gather | solution.py:115
  730.7 113.8 %all-gather.23.cloned.1.call-done = bf16[2048,2048]{1,0:T(8,128)(2,1)} async-done(((bf16[2048,256]{1,0:T(8,128)(2,1)}), bf16[2048,2048]{1,0:T(8,128)(2,1)}) %all-gather.23.cloned.1.call-update) | async-done | bytes 8388624 | tf_op jit(solution)/shard_map/all_gather | solution.py:116
  856.4 83.6 %all-reduce.12.cloned.1.call-done = f32[512,2048]{1,0:T(8,128)} async-done(((f32[512,2048]{1,0:T(8,128)}), f32[512,2048]{1,0:T(8,128)}) %all-reduce.12.cloned.1.call-update) | async-done | bytes 4194320 | tf_op jit(solution)/shard_map/psum | solution.py:26
  969.7 85.5 %all-reduce.14.cloned.1.call-done = f32[512,2048]{1,0:T(8,128)} async-done(((f32[512,2048]{1,0:T(8,128)}), f32[512,2048]{1,0:T(8,128)}) %all-reduce.14.cloned.1.call-update) | async-done | bytes 4194320 | tf_op jit(solution)/shard_map/psum | solution.py:30
  1072.5 85.2 %all-reduce.16.cloned.1.call-done = f32[512,2048]{1,0:T(8,128)} async-done(((f32[512,2048]{1,0:T(8,128)}), f32[512,2048]{1,0:T(8,128)}) %all-reduce.16.cloned.1.call-update) | async-done | bytes 4194320 | tf_op jit(solution)/shard_map/psum | solution.py:30
  1218.7 12.4 convolution_convert_fusion
  1260.7 16.9 all-reduce.18.cloned.1.call-done
  1283.1 38.6 %all-reduce = (bf16[4,2048]{1,0:T(4,128)(2,1)S(1)}, bf16[4,2048]{1,0:T(4,128)(2,1)S(1)}, bf16[3,2048]{1,0:T(4,128)(2,1)S(1)}, bf16[2048]{0:T(1024)(128)(2,1)S(1)}) all-reduce(bf16[4,2048]{1,0:T(4,128)(2,1)S(1)} %get-tuple-element.190, bf16[4,2048]{1,0:T(4,128)(2,1)S(1)} %get-tuple-element.191, ...), channel_id=1, replica_groups=mesh['dp'=8,'mp'=4] {'dp'}, use_global_device_ids=true, to_apply=%region_40.41 | all-reduce | flops 24576 | bytes 98304 | tf_op jit(solution)/shard_map/psum | solution.py:249
  1329.8 20.3 reduce-scatter.15.cloned.1.call-done
  1352.0 31.5 %reduce-scatter.9.cloned.1.call-done = bf16[256,1024]{1,0:T(8,128)(2,1)} async-done(((bf16[256,4096]{1,0:T(8,128)(2,1)}), bf16[256,1024]{1,0:T(8,128)(2,1)}) %reduce-scatter.9.cloned.1.call-update) | async-done | bytes 524304 | tf_op jit(solution)/shard_map/reduce_scatter | solution.py:207
  1385.6 70.2 %reduce-scatter.19.cloned.1.call-done = bf16[512,256]{1,0:T(8,128)(2,1)} async-done(((bf16[512,2048]{1,0:T(8,128)(2,1)}), bf16[512,256]{1,0:T(8,128)(2,1)}) %reduce-scatter.19.cloned.1.call-update) | async-done | bytes 262160 | tf_op jit(solution)/shard_map/reduce_scatter | solution.py:267
  1457.5 70.0 %reduce-scatter.13.cloned.1.call-done = bf16[512,256]{1,0:T(8,128)(2,1)} async-done(((bf16[512,2048]{1,0:T(8,128)(2,1)}), bf16[512,256]{1,0:T(8,128)(2,1)}) %reduce-scatter.13.cloned.1.call-update) | async-done | bytes 262160 | tf_op jit(solution)/shard_map/reduce_scatter | solution.py:258
  1529.3 148.7 %reduce-scatter.23.cloned.1.call-done = bf16[2048,256]{1,0:T(8,128)(2,1)} async-done(((bf16[2048,2048]{1,0:T(8,128)(2,1)}), bf16[2048,256]{1,0:T(8,128)(2,1)}) %reduce-scatter.23.cloned.1.call-update) | async-done | bytes 1048592 | tf_op jit(solution)/shard_map/reduce_scatter | solution.py:273
  1680.8 147.4 %reduce-scatter.21.cloned.1.call-done = bf16[256,2048]{1,0:T(8,128)(2,1)} async-done(((bf16[2048,2048]{1,0:T(8,128)(2,1)}), bf16[256,2048]{1,0:T(8,128)(2,1)}) %reduce-scatter.21.cloned.1.call-update) | async-done | bytes 1048592 | tf_op jit(solution)/shard_map/reduce_scatter | solution.py:270
  1830.9 118.5 %reduce-scatter.11.cloned.1.call-done = bf16[3,256,512]{1,2,0:T(8,128)(2,1)} async-done(((bf16[3,2048,512]{1,2,0:T(8,128)(2,1)}), bf16[3,256,512]{1,2,0:T(8,128)(2,1)}) %reduce-scatter.11.cloned.1.call-update) | async-done | bytes 786448 | tf_op jit(solution)/shard_map/reduce_scatter | solution.py:255
  1951.9 148.2 %reduce-scatter.17.cloned.1.call-done = bf16[2,512,512]{1,2,0:T(8,128)(2,1)} async-done(((bf16[2,4096,512]{1,2,0:T(8,128)(2,1)}), bf16[2,512,512]{1,2,0:T(8,128)(2,1)}) %reduce-scatter.17.cloned.1.call-update) | async-done | bytes 1048592 | tf_op jit(solution)/shard_map/reduce_scatter | solution.py:264
  (273 shorter events, 247.6 us)
Async XLA Ops:
  7.2 105.7 %all-gather.9.cloned.1.call-start = ((), (), s32[]{:S(2)}) async-start(), calls=%async_computation.8 | async-start | bytes 7077888 | tf_op jit(solution)/shard_map/all_gather | solution.py:110
  9.7 153.8 %all-gather.11.cloned.1.call-start = ((), (), s32[]{:S(2)}) async-start(), calls=%async_computation.9 | async-start | bytes 2359296 | tf_op jit(solution)/shard_map/all_gather | solution.py:111
  10.5 241.7 %all-reduce.8.cloned.1.call-start = ((), (), s32[]{:S(2)}) async-start(), calls=%async_computation.10 | async-start | bytes 8388608 | tf_op jit(solution)/shard_map/psum | solution.py:26
  168.4 135.1 %all-gather.17.cloned.1.call-start = ((), (), s32[]{:S(2)}) async-start(), calls=%async_computation.13 | async-start | bytes 2359296 | tf_op jit(solution)/shard_map/all_gather | solution.py:112
  169.0 157.0 %all-gather.15.cloned.1.call-start = ((), (), s32[]{:S(2)}) async-start(), calls=%async_computation.12 | async-start | bytes 2621440 | tf_op jit(solution)/shard_map/all_gather | solution.py:119
  169.6 283.9 %all-gather.13.cloned.1.call-start = ((), (), s32[]{:S(2)}) async-start(), calls=%async_computation.11 | async-start | bytes 9437184 | tf_op jit(solution)/shard_map/all_gather | solution.py:113
  171.0 333.1 %all-gather.19.cloned.1.call-start = ((), (), s32[]{:S(2)}) async-start(), calls=%async_computation.14 | async-start | bytes 2359296 | tf_op jit(solution)/shard_map/all_gather | solution.py:114
  171.7 421.0 %all-reduce.10.cloned.1.call-start = ((), (), s32[]{:S(2)}) async-start(), calls=%async_computation.15 | async-start | bytes 8388608 | tf_op jit(solution)/shard_map/psum | solution.py:26
  306.4 153.5 %copy-start.26 = (bf16[512,512]{0,1:T(8,128)(2,1)}, bf16[512,512]{0,1:T(8,128)(2,1)S(1)}, u32[]{:S(2)}) copy-start(bf16[512,512]{0,1:T(8,128)(2,1)S(1)} %convolution_convert_fusion.9) | copy-start | bytes 1572868
  508.9 210.6 %all-gather.21.cloned.1.call-start = ((), (), s32[]{:S(2)}) async-start(), calls=%async_computation.16 | async-start | bytes 9437184 | tf_op jit(solution)/shard_map/all_gather | solution.py:115
  509.7 334.9 %all-gather.23.cloned.1.call-start = ((), (), s32[]{:S(2)}) async-start(), calls=%async_computation.17 | async-start | bytes 9437184 | tf_op jit(solution)/shard_map/all_gather | solution.py:116
  510.2 429.7 %all-reduce.12.cloned.1.call-start = ((), (), s32[]{:S(2)}) async-start(), calls=%async_computation.18 | async-start | bytes 8388608 | tf_op jit(solution)/shard_map/psum | solution.py:26
  719.5 125.0 %copy-start.51 = (f32[2048]{0:T(1024)S(1)}, f32[2048]{0:T(1024)}, u32[]{:S(2)}) copy-start(f32[2048]{0:T(1024)} %param.30) | copy-start | bytes 24580
  856.1 199.1 %all-reduce.14.cloned.1.call-start = ((), (), s32[]{:S(2)}) async-start(), calls=%async_computation.19 | async-start | bytes 8388608 | tf_op jit(solution)/shard_map/psum | solution.py:30
  969.4 188.3 %all-reduce.16.cloned.1.call-start = ((), (), s32[]{:S(2)}) async-start(), calls=%async_computation.20 | async-start | bytes 8388608 | tf_op jit(solution)/shard_map/psum | solution.py:30
  1071.9 205.7 %all-reduce.18.cloned.1.call-start = ((), (), s32[]{:S(2)}) async-start(), calls=%async_computation.21 | async-start | bytes 8388608 | tf_op jit(solution)/shard_map/psum | solution.py:30
  1191.8 158.3 %reduce-scatter.15.cloned.1.call-start = ((), (), s32[]{:S(2)}) async-start(), calls=%async_computation.25 | async-start | bytes 2359296 | tf_op jit(solution)/shard_map/reduce_scatter | solution.py:261
  1196.2 187.2 %reduce-scatter.9.cloned.1.call-start = ((), (), s32[]{:S(2)}) async-start(), calls=%async_computation.22 | async-start | bytes 2621440 | tf_op jit(solution)/shard_map/reduce_scatter | solution.py:207
  1208.7 247.0 %reduce-scatter.19.cloned.1.call-start = ((), (), s32[]{:S(2)}) async-start(), calls=%async_computation.27 | async-start | bytes 2359296 | tf_op jit(solution)/shard_map/reduce_scatter | solution.py:267
  1213.7 313.9 %reduce-scatter.13.cloned.1.call-start = ((), (), s32[]{:S(2)}) async-start(), calls=%async_computation.24 | async-start | bytes 2359296 | tf_op jit(solution)/shard_map/reduce_scatter | solution.py:258
  1218.6 459.5 %reduce-scatter.23.cloned.1.call-start = ((), (), s32[]{:S(2)}) async-start(), calls=%async_computation.29 | async-start | bytes 9437184 | tf_op jit(solution)/shard_map/reduce_scatter | solution.py:273
  1231.1 597.1 %reduce-scatter.21.cloned.1.call-start = ((), (), s32[]{:S(2)}) async-start(), calls=%async_computation.28 | async-start | bytes 9437184 | tf_op jit(solution)/shard_map/reduce_scatter | solution.py:270
  1242.2 707.2 %reduce-scatter.11.cloned.1.call-start = ((), (), s32[]{:S(2)}) async-start(), calls=%async_computation.23 | async-start | bytes 7077888 | tf_op jit(solution)/shard_map/reduce_scatter | solution.py:255
  1251.2 849.0 %reduce-scatter.17.cloned.1.call-start = ((), (), s32[]{:S(2)}) async-start(), calls=%async_computation.26 | async-start | bytes 9437184 | tf_op jit(solution)/shard_map/reduce_scatter | solution.py:264
  (55 other events, 751.6 us)
Sparse Core Ops, SparseCore 0:
  10.6 102.1 all-gather.8
  114.9 48.5 all-gather.10
  168.5 83.6 all-reduce.7
  254.2 49.2 all-gather.16
  304.9 21.0 all-gather.14
  328.5 124.9 all-gather.12
  455.5 48.5 all-gather.18
  509.0 83.6 all-reduce.9
  594.9 124.6 all-gather.20
  721.4 123.1 all-gather.22
  856.2 83.6 all-reduce.11
  969.5 85.6 all-reduce.13
  1072.1 85.6 all-reduce.15
  1191.9 85.6 all-reduce.17
  1281.5 68.5 reduce-scatter.14
  1353.1 30.2 reduce-scatter.8
  1386.8 68.8 reduce-scatter.18
  1459.7 67.8 reduce-scatter.12
  1531.2 146.8 reduce-scatter.22
  1681.6 146.5 reduce-scatter.20
  1831.8 117.5 reduce-scatter.10
  1953.0 147.0 reduce-scatter.16
where the time goes:
time: 2120 us; the launch traced here: 2110 us
  waiting for transfers between devices  1800 us (85%)
  matrix products  151 us (7%)
  other arithmetic  65.1 us (3%)
  blocking collectives  38.6 us (2%)
  local copies, waits for them, and re-layouts  36.8 us (2%)
    psum x3, waiting for transfers between devices, heads_sum(): return lax.psum(partial_value, 'mp')  246 us
    psum x3, waiting for transfers between devices, input_sum(): return lax.psum(partial_value, 'mp')  188 us
    reduce_scatter x1, waiting for transfers between devices, on_device(): lax.psum_scatter(grad_down.astype(jnp.bfloat16), 'dp', scatter_dimension=...  149 us
    reduce_scatter x1, waiting for transfers between devices, on_device(): lax.psum_scatter(grad_ckv.astype(jnp.bfloat16), 'dp', scatter_dimension=1...  148 us
    reduce_scatter x1, waiting for transfers between devices, on_device(): lax.psum_scatter(grad_up.astype(jnp.bfloat16), 'dp', scatter_dimension=0,...  147 us
    all_gather x1, waiting for transfers between devices, on_device(): lax.all_gather(c_kv, 'dp', axis=1, tiled=True)  127 us
    all_gather x1, waiting for transfers between devices, on_device(): lax.all_gather(w_up, 'dp', axis=0, tiled=True)  120 us
    reduce_scatter x1, waiting for transfers between devices, on_device(): lax.psum_scatter(grad_qkv.astype(jnp.bfloat16), 'dp', scatter_dimension=1...  118 us
  transfers between devices with their start and end apart: 22, of which 22 were waited for; matrix products, arithmetic and copies ran while one was open for 7% of the time, Pallas kernels for 0%

commit v1 on v0

--- a/solution.py
+++ b/solution.py
@@ -27,7 +27,7 @@
 
 
 def input_sum(partial_value):
-    return lax.psum(partial_value, "mp")
+    return jnp.sum(lax.all_gather(partial_value, "mp"), axis=0)
 
 
 def split_heads(values):

time: 2120 us -> 2220 us (1.047)
  other arithmetic: 65.1 us -> 116 us
  waiting for transfers between devices: 1800 us -> 1850 us
    all_gather x0 -> x3, waiting for transfers between devices: none -> 262 us  [input_sum(): return jnp.sum(lax.all_gather(partial_value, 'mp'), axis=0)]
    psum x3 -> x0, waiting for transfers between devices: 188 us -> none  [input_sum(): return lax.psum(partial_value, 'mp')]
    reduce_scatter x1, waiting for transfers between devices: 149 us -> 91.6 us  [on_device(): lax.psum_scatter(grad_down.astype(jnp.bfloat16), 'dp', scatter_dimension=...]
    reduce_scatter x1, waiting for transfers between devices: 20.3 us -> 61.4 us  [on_device(): lax.psum_scatter(grad_cq.astype(jnp.bfloat16), 'dp', scatter_dimension=0,...]
    reduce_sum x0 -> x3, other arithmetic: none -> 30.5 us  [input_sum(): return jnp.sum(lax.all_gather(partial_value, 'mp'), axis=0)]
  transfers between devices with their start and end apart: 22 -> 22, of which waited for: 22 -> 22; matrix products, arithmetic and copies ran while one was open for 7% -> 8% of each run, Pallas kernels for 0% -> 0%
where the time goes in v1:
time: 2220 us; the launch traced here: 2210 us
  waiting for transfers between devices  1850 us (83%)
  matrix products  156 us (7%)
  other arithmetic  116 us (5%)
  blocking collectives  37.6 us (2%)
  local copies, waits for them, and re-layouts  32.3 us (1%)
    all_gather x3, waiting for transfers between devices, input_sum(): return jnp.sum(lax.all_gather(partial_value, 'mp'), axis=0)  262 us
    psum x3, waiting for transfers between devices, heads_sum(): return lax.psum(partial_value, 'mp')  246 us
    reduce_scatter x1, waiting for transfers between devices, on_device(): lax.psum_scatter(grad_ckv.astype(jnp.bfloat16), 'dp', scatter_dimension=1...  149 us
    reduce_scatter x1, waiting for transfers between devices, on_device(): lax.psum_scatter(grad_up.astype(jnp.bfloat16), 'dp', scatter_dimension=0,...  147 us
    all_gather x1, waiting for transfers between devices, on_device(): lax.all_gather(c_kv, 'dp', axis=1, tiled=True)  127 us
    all_gather x1, waiting for transfers between devices, on_device(): lax.all_gather(w_up, 'dp', axis=0, tiled=True)  120 us
    reduce_scatter x1, waiting for transfers between devices, on_device(): lax.psum_scatter(grad_qkv.astype(jnp.bfloat16), 'dp', scatter_dimension=1...  119 us
    all_gather x1, waiting for transfers between devices, on_device(): lax.all_gather(w_down, 'dp', axis=1, tiled=True)  114 us
  transfers between devices with their start and end apart: 22, of which 22 were waited for; matrix products, arithmetic and copies ran while one was open for 8% of the time, Pallas kernels for 0%

profile of v1, /device:TPU:0, one launch (start us, length us, event | category | flops | bytes accessed | tf_op | source)
XLA Modules:
  0.0 2212.6 jit_solution(759549742026464051)
XLA Ops:
  13.5 99.3 %all-gather.15.cloned.1.call-done = bf16[3,2048,512]{1,2,0:T(8,128)(2,1)} async-done(((bf16[3,256,512]{1,2,0:T(8,128)(2,1)}), bf16[3,2048,512]{1,2,0:T(8,128)(2,1)}) %all-gather.15.cloned.1.call-update) | async-done | bytes 6291472 | tf_op jit(solution)/shard_map/all_gather | solution.py:110
  124.4 39.1 %all-gather.17.cloned.1.call-done = bf16[512,2048]{1,0:T(8,128)(2,1)} async-done(((bf16[512,256]{1,0:T(8,128)(2,1)}), bf16[512,2048]{1,0:T(8,128)(2,1)}) %all-gather.17.cloned.1.call-update) | async-done | bytes 2097168 | tf_op jit(solution)/shard_map/all_gather | solution.py:111
  172.1 80.1 %all-reduce.5.cloned.1.call-done = f32[512,2048]{1,0:T(8,128)} async-done(((f32[512,2048]{1,0:T(8,128)}), f32[512,2048]{1,0:T(8,128)}) %all-reduce.5.cloned.1.call-update) | async-done | bytes 4194320 | tf_op jit(solution)/shard_map/psum | solution.py:26
  257.8 45.6 %all-gather.23.cloned.1.call-done = bf16[2048,512]{1,0:T(8,128)(2,1)} async-done(((bf16[256,512]{1,0:T(8,128)(2,1)}), bf16[2048,512]{1,0:T(8,128)(2,1)}) %all-gather.23.cloned.1.call-update) | async-done | bytes 2097168 | tf_op jit(solution)/shard_map/all_gather | solution.py:112
  306.4 19.6 all-gather.21.cloned.1.call-done
  326.0 127.4 %all-gather.19.cloned.1.call-done = bf16[2,4096,512]{1,2,0:T(8,128)(2,1)} async-done(((bf16[2,512,512]{1,2,0:T(8,128)(2,1)}), bf16[2,4096,512]{1,2,0:T(8,128)(2,1)}) %all-gather.19.cloned.1.call-update) | async-done | bytes 8388624 | tf_op jit(solution)/shard_map/all_gather | solution.py:113
  461.3 42.8 %all-gather.25.cloned.1.call-done = bf16[512,2048]{1,0:T(8,128)(2,1)} async-done(((bf16[512,256]{1,0:T(8,128)(2,1)}), bf16[512,2048]{1,0:T(8,128)(2,1)}) %all-gather.25.cloned.1.call-update) | async-done | bytes 2097168 | tf_op jit(solution)/shard_map/all_gather | solution.py:114
  510.5 82.2 %all-reduce.7.cloned.1.call-done = f32[512,2048]{1,0:T(8,128)} async-done(((f32[512,2048]{1,0:T(8,128)}), f32[512,2048]{1,0:T(8,128)}) %all-reduce.7.cloned.1.call-update) | async-done | bytes 4194320 | tf_op jit(solution)/shard_map/psum | solution.py:26
  599.3 120.2 %all-gather.27.cloned.1.call-done = bf16[2048,2048]{1,0:T(8,128)(2,1)} async-done(((bf16[256,2048]{1,0:T(8,128)(2,1)}), bf16[2048,2048]{1,0:T(8,128)(2,1)}) %all-gather.27.cloned.1.call-update) | async-done | bytes 8388624 | tf_op jit(solution)/shard_map/all_gather | solution.py:115
  730.7 113.9 %all-gather.29.cloned.1.call-done = bf16[2048,2048]{1,0:T(8,128)(2,1)} async-done(((bf16[2048,256]{1,0:T(8,128)(2,1)}), bf16[2048,2048]{1,0:T(8,128)(2,1)}) %all-gather.29.cloned.1.call-update) | async-done | bytes 8388624 | tf_op jit(solution)/shard_map/all_gather | solution.py:116
  856.5 83.5 %all-reduce.9.cloned.1.call-done = f32[512,2048]{1,0:T(8,128)} async-done(((f32[512,2048]{1,0:T(8,128)}), f32[512,2048]{1,0:T(8,128)}) %all-reduce.9.cloned.1.call-update) | async-done | bytes 4194320 | tf_op jit(solution)/shard_map/psum | solution.py:26
  970.6 105.7 %all-gather.31.cloned.1.call-done = f32[2048,2048]{1,0:T(8,128)} async-done(((f32[512,2048]{1,0:T(8,128)}), f32[2048,2048]{1,0:T(8,128)}) %all-gather.31.cloned.1.call-update) | async-done | bytes 16777232 | tf_op jit(solution)/shard_map/all_gather | solution.py:30
  1103.4 13.4 convolution_convert_fusion
  1157.5 51.8 %all-gather.33.cloned.1.call-done = f32[2048,2048]{1,0:T(8,128)} async-done(((f32[512,2048]{1,0:T(8,128)}), f32[2048,2048]{1,0:T(8,128)}) %all-gather.33.cloned.1.call-update) | async-done | bytes 16777232 | tf_op jit(solution)/shard_map/all_gather | solution.py:30
  1269.0 91.6 %reduce-scatter.23.cloned.1.call-done = bf16[2048,256]{1,0:T(8,128)(2,1)} async-done(((bf16[2048,2048]{1,0:T(8,128)(2,1)}), bf16[2048,256]{1,0:T(8,128)(2,1)}) %reduce-scatter.23.cloned.1.call-update) | async-done | bytes 1048592 | tf_op jit(solution)/shard_map/reduce_scatter | solution.py:273
  1363.3 147.4 %reduce-scatter.21.cloned.1.call-done = bf16[256,2048]{1,0:T(8,128)(2,1)} async-done(((bf16[2048,2048]{1,0:T(8,128)(2,1)}), bf16[256,2048]{1,0:T(8,128)(2,1)}) %reduce-scatter.21.cloned.1.call-update) | async-done | bytes 1048592 | tf_op jit(solution)/shard_map/reduce_scatter | solution.py:270
  1520.2 61.4 %reduce-scatter.15.cloned.1.call-done = bf16[256,512]{1,0:T(8,128)(2,1)} async-done(((bf16[2048,512]{1,0:T(8,128)(2,1)}), bf16[256,512]{1,0:T(8,128)(2,1)}) %reduce-scatter.15.cloned.1.call-update) | async-done | bytes 262160 | tf_op jit(solution)/shard_map/reduce_scatter | solution.py:261
  1583.3 31.5 %reduce-scatter.9.cloned.1.call-done = bf16[256,1024]{1,0:T(8,128)(2,1)} async-done(((bf16[256,4096]{1,0:T(8,128)(2,1)}), bf16[256,1024]{1,0:T(8,128)(2,1)}) %reduce-scatter.9.cloned.1.call-update) | async-done | bytes 524304 | tf_op jit(solution)/shard_map/reduce_scatter | solution.py:207
  1616.9 70.3 %reduce-scatter.19.cloned.1.call-done = bf16[512,256]{1,0:T(8,128)(2,1)} async-done(((bf16[512,2048]{1,0:T(8,128)(2,1)}), bf16[512,256]{1,0:T(8,128)(2,1)}) %reduce-scatter.19.cloned.1.call-update) | async-done | bytes 262160 | tf_op jit(solution)/shard_map/reduce_scatter | solution.py:267
  1689.0 148.9 %reduce-scatter.17.cloned.1.call-done = bf16[2,512,512]{1,2,0:T(8,128)(2,1)} async-done(((bf16[2,4096,512]{1,2,0:T(8,128)(2,1)}), bf16[2,512,512]{1,2,0:T(8,128)(2,1)}) %reduce-scatter.17.cloned.1.call-update) | async-done | bytes 1048592 | tf_op jit(solution)/shard_map/reduce_scatter | solution.py:264
  1847.3 62.0 %reduce-scatter.13.cloned.1.call-done = bf16[512,256]{1,0:T(8,128)(2,1)} async-done(((bf16[512,2048]{1,0:T(8,128)(2,1)}), bf16[512,256]{1,0:T(8,128)(2,1)}) %reduce-scatter.13.cloned.1.call-update) | async-done | bytes 262160 | tf_op jit(solution)/shard_map/reduce_scatter | solution.py:258
  1911.1 119.4 %reduce-scatter.11.cloned.1.call-done = bf16[3,256,512]{1,2,0:T(8,128)(2,1)} async-done(((bf16[3,2048,512]{1,2,0:T(8,128)(2,1)}), bf16[3,256,512]{1,2,0:T(8,128)(2,1)}) %reduce-scatter.11.cloned.1.call-update) | async-done | bytes 786448 | tf_op jit(solution)/shard_map/reduce_scatter | solution.py:255
  2033.0 104.2 %all-gather.35.cloned.1.call-done = f32[2048,2048]{1,0:T(8,128)} async-done(((f32[512,2048]{1,0:T(8,128)}), f32[2048,2048]{1,0:T(8,128)}) %all-gather.35.cloned.1.call-update) | async-done | bytes 16777232 | tf_op jit(solution)/shard_map/all_gather | solution.py:30
  2165.5 37.6 %all-reduce = (bf16[4,2048]{1,0:T(4,128)(2,1)S(1)}, bf16[4,2048]{1,0:T(4,128)(2,1)S(1)}, bf16[3,2048]{1,0:T(4,128)(2,1)S(1)}, bf16[2048]{0:T(1024)(128)(2,1)S(1)}) all-reduce(bf16[4,2048]{1,0:T(4,128)(2,1)S(1)} %get-tuple-element.186, bf16[4,2048]{1,0:T(4,128)(2,1)S(1)} %get-tuple-element.187, ...), channel_id=1, replica_groups=mesh['dp'=8,'mp'=4] {'dp'}, use_global_device_ids=true, to_apply=%region_40.41 | all-reduce | flops 24576 | bytes 98304 | tf_op jit(solution)/shard_map/psum | solution.py:249
  (313 shorter events, 298.3 us)
Async XLA Ops:
  7.2 105.7 %all-gather.15.cloned.1.call-start = ((), (), s32[]{:S(2)}) async-start(), calls=%async_computation.8 | async-start | bytes 7077888 | tf_op jit(solution)/shard_map/all_gather | solution.py:110
  9.7 153.8 %all-gather.17.cloned.1.call-start = ((), (), s32[]{:S(2)}) async-start(), calls=%async_computation.9 | async-start | bytes 2359296 | tf_op jit(solution)/shard_map/all_gather | solution.py:111
  10.5 241.7 %all-reduce.5.cloned.1.call-start = ((), (), s32[]{:S(2)}) async-start(), calls=%async_computation.10 | async-start | bytes 8388608 | tf_op jit(solution)/shard_map/psum | solution.py:26
  13.5 242.1 %copy-start.43 = (f32[1,2048]{1,0:T(1,128)}, f32[1,2048]{1,0:T(1,128)S(1)}, u32[]{:S(2)}) copy-start(f32[1,2048]{1,0:T(1,128)S(1)} %get-tuple-element.166) | copy-start | bytes 24580
  168.4 135.1 %all-gather.23.cloned.1.call-start = ((), (), s32[]{:S(2)}) async-start(), calls=%async_computation.13 | async-start | bytes 2359296 | tf_op jit(solution)/shard_map/all_gather | solution.py:112
  169.0 157.0 %all-gather.21.cloned.1.call-start = ((), (), s32[]{:S(2)}) async-start(), calls=%async_computation.12 | async-start | bytes 2621440 | tf_op jit(solution)/shard_map/all_gather | solution.py:119
  169.6 283.9 %all-gather.19.cloned.1.call-start = ((), (), s32[]{:S(2)}) async-start(), calls=%async_computation.11 | async-start | bytes 9437184 | tf_op jit(solution)/shard_map/all_gather | solution.py:113
  171.0 333.1 %all-gather.25.cloned.1.call-start = ((), (), s32[]{:S(2)}) async-start(), calls=%async_computation.14 | async-start | bytes 2359296 | tf_op jit(solution)/shard_map/all_gather | solution.py:114
  171.7 421.0 %all-reduce.7.cloned.1.call-start = ((), (), s32[]{:S(2)}) async-start(), calls=%async_computation.15 | async-start | bytes 8388608 | tf_op jit(solution)/shard_map/psum | solution.py:26
  306.4 153.5 %copy-start.28 = (bf16[512,512]{0,1:T(8,128)(2,1)}, bf16[512,512]{0,1:T(8,128)(2,1)S(1)}, u32[]{:S(2)}) copy-start(bf16[512,512]{0,1:T(8,128)(2,1)S(1)} %convolution_convert_fusion.9) | copy-start | bytes 1572868
  508.9 210.6 %all-gather.27.cloned.1.call-start = ((), (), s32[]{:S(2)}) async-start(), calls=%async_computation.16 | async-start | bytes 9437184 | tf_op jit(solution)/shard_map/all_gather | solution.py:115
  509.7 334.9 %all-gather.29.cloned.1.call-start = ((), (), s32[]{:S(2)}) async-start(), calls=%async_computation.17 | async-start | bytes 9437184 | tf_op jit(solution)/shard_map/all_gather | solution.py:116
  510.2 429.7 %all-reduce.9.cloned.1.call-start = ((), (), s32[]{:S(2)}) async-start(), calls=%async_computation.18 | async-start | bytes 8388608 | tf_op jit(solution)/shard_map/psum | solution.py:26
  856.1 220.1 %all-gather.31.cloned.1.call-start = ((), (), s32[]{:S(2)}) async-start(), calls=%async_computation.27 | async-start | bytes 20971520 | tf_op jit(solution)/shard_map/all_gather | solution.py:30
  970.0 239.2 %all-gather.33.cloned.1.call-start = ((), (), s32[]{:S(2)}) async-start(), calls=%async_computation.28 | async-start | bytes 20971520 | tf_op jit(solution)/shard_map/all_gather | solution.py:30
  1103.2 257.4 %reduce-scatter.23.cloned.1.call-start = ((), (), s32[]{:S(2)}) async-start(), calls=%async_computation.26 | async-start | bytes 9437184 | tf_op jit(solution)/shard_map/reduce_scatter | solution.py:273
  1116.8 393.9 %reduce-scatter.21.cloned.1.call-start = ((), (), s32[]{:S(2)}) async-start(), calls=%async_computation.25 | async-start | bytes 9437184 | tf_op jit(solution)/shard_map/reduce_scatter | solution.py:270
  1129.6 451.9 %reduce-scatter.15.cloned.1.call-start = ((), (), s32[]{:S(2)}) async-start(), calls=%async_computation.22 | async-start | bytes 2359296 | tf_op jit(solution)/shard_map/reduce_scatter | solution.py:261
  1134.1 480.7 %reduce-scatter.9.cloned.1.call-start = ((), (), s32[]{:S(2)}) async-start(), calls=%async_computation.19 | async-start | bytes 2621440 | tf_op jit(solution)/shard_map/reduce_scatter | solution.py:207
  1146.7 540.5 %reduce-scatter.19.cloned.1.call-start = ((), (), s32[]{:S(2)}) async-start(), calls=%async_computation.24 | async-start | bytes 2359296 | tf_op jit(solution)/shard_map/reduce_scatter | solution.py:267
  1151.7 686.1 %reduce-scatter.17.cloned.1.call-start = ((), (), s32[]{:S(2)}) async-start(), calls=%async_computation.23 | async-start | bytes 9437184 | tf_op jit(solution)/shard_map/reduce_scatter | solution.py:264
  1157.4 751.9 %reduce-scatter.13.cloned.1.call-start = ((), (), s32[]{:S(2)}) async-start(), calls=%async_computation.21 | async-start | bytes 2359296 | tf_op jit(solution)/shard_map/reduce_scatter | solution.py:258
  1233.2 797.2 %reduce-scatter.11.cloned.1.call-start = ((), (), s32[]{:S(2)}) async-start(), calls=%async_computation.20 | async-start | bytes 7077888 | tf_op jit(solution)/shard_map/reduce_scatter | solution.py:255
  1257.4 879.8 %all-gather.35.cloned.1.call-start = ((), (), s32[]{:S(2)}) async-start(), calls=%async_computation.29 | async-start | bytes 20971520 | tf_op jit(solution)/shard_map/all_gather | solution.py:30
  (72 other events, 1143.7 us)
Sparse Core Ops, SparseCore 0:
  10.6 102.1 all-gather.14
  114.9 48.5 all-gather.16
  168.5 83.6 all-reduce.4
  254.2 49.2 all-gather.22
  304.9 21.0 all-gather.20
  328.5 124.9 all-gather.18
  455.5 48.5 all-gather.24
  509.0 83.6 all-reduce.6
  594.9 124.6 all-gather.26
  721.4 123.1 all-gather.28
  856.3 83.6 all-reduce.8
  970.2 106.0 all-gather.30
  1103.3 105.8 all-gather.32
  1212.7 147.8 reduce-scatter.22
  1364.1 146.5 reduce-scatter.20
  1514.1 67.3 reduce-scatter.14
  1584.5 30.2 reduce-scatter.8
  1618.2 68.9 reduce-scatter.18
  1690.8 146.9 reduce-scatter.16
  1841.2 67.9 reduce-scatter.12
  1912.9 117.4 reduce-scatter.10
  2032.0 105.1 all-gather.34
